TPU v7x, 32 devices: a whole 2x2x4 slice. The times are simulated.
32 devices in a mesh: row: 8 (over z, y), col: 4 (over x, core).
Axes of the slice: x: 2, y: 2, z: 4, core: 2. Of those that a mesh axis runs over, the one named last changes fastest.
Arguments:
- tensor_ri: bfloat16 [8, 8, 4, 128, 1152], P('row', None, 'col'), may hold values from -6 to 6
- block_mask: int32 [8, 4, 9], P('row', 'col'), may hold values 0 or 1
- green_virt: bfloat16 [8, 4, 128, 3200], P('row', 'col'), may hold values from -0.1875 to 0.1875
- green_occ: bfloat16 [8, 4, 128, 128], P('row', 'col'), may hold values from -0.5 to 0.5
Outputs:
- response: float32 [8, 8], replicated
All inputs are finite; a program needn't handle non-finite values. No bound on the sum of `block_mask` on one device may be relied on, other than what follows from the above.
Results may differ from a plain program's by a relative error of at most 0.0044.
Values may be sent and summed in bfloat16 or wider, within the bound.
A program may use at most 192 MiB of HBM per device.

v0:
```python
import math

import jax
import jax.numpy as jnp
from jax import lax
from jax.sharding import PartitionSpec as P


def extended(cells, sides, width):
    for axis, dim in sides:
        count = lax.axis_size(axis)
        ends = count - 1
        head = lax.slice_in_dim(cells, 0, width, axis=dim)
        tail = lax.slice_in_dim(cells, cells.shape[dim] - width, cells.shape[dim], axis=dim)
        cells = jnp.concatenate(
            [
                lax.ppermute(tail, axis, [(i, (i + 1) % count) for i in range(ends)]),
                cells,
                lax.ppermute(head, axis, [((i + 1) % count, i) for i in range(ends)]),
            ],
            axis=dim,
        )
    return cells


def window_of(band, src_row, src_col, block_width):
    grid_band = band.reshape(block_width, 5, 5, block_width)
    picked = grid_band[:, 2 - src_row : 5 - src_row, 2 - src_col : 5 - src_col, :]
    return picked.reshape(block_width, 9 * block_width)


def per_device(tensor_ri, block_mask, green_virt, green_occ):
    row_count = lax.axis_size("row")
    col_count = lax.axis_size("col")
    block_width = green_occ.shape[-1]
    pair_width = tensor_ri.shape[-1]
    occ_block = green_occ[0, 0]
    regrouped = lax.all_to_all(tensor_ri, "row", split_axis=1, concat_axis=0, tiled=True)
    occ_applied = jnp.einsum(
        "ji,pabiw->pabjw", occ_block, regrouped, preferred_element_type=jnp.float32
    ).astype(jnp.bfloat16)
    rows_all = regrouped.shape[0]
    regrouped = regrouped.reshape(rows_all, block_width, pair_width)
    occ_applied = occ_applied.reshape(rows_all, block_width, pair_width)
    grid_row = lax.axis_index("row")
    grid_col = lax.axis_index("col")
    slots = jnp.arange(9, dtype=jnp.int32)
    near_row = grid_row + slots // 3 - 1
    near_col = grid_col + slots % 3 - 1
    usable = (
        (block_mask[0, 0] == 1)
        & (near_row >= 0)
        & (near_row < row_count)
        & (near_col >= 0)
        & (near_col < col_count)
    )
    kept_slots = jnp.repeat(usable.astype(jnp.bfloat16), block_width)
    regrouped = regrouped * kept_slots
    occ_applied = occ_applied * kept_slots
    windows = []
    rim_blocks = extended(green_virt, (("row", 0), ("col", 1)), 1)
    for source in range(9):
        src_row, src_col = (source // 3, source % 3)
        windows.append(window_of(rim_blocks[src_row, src_col], src_row, src_col, block_width))
    flat_rows = regrouped.reshape(rows_all * block_width, pair_width)
    half_sum = jnp.zeros((rows_all * block_width, pair_width), jnp.float32)
    for source in range(9):
        tile = flat_rows[:, source * block_width : (source + 1) * block_width]
        half_sum = half_sum + jnp.dot(tile, windows[source], preferred_element_type=jnp.float32)
    half_done = half_sum.astype(jnp.bfloat16).reshape(rows_all, block_width * pair_width)
    occ_flat = occ_applied.reshape(rows_all, block_width * pair_width)
    partial_value = lax.dot_general(
        half_done, occ_flat, (((1,), (1,)), ((), ())), preferred_element_type=jnp.float32
    )
    total_basis = block_width * row_count * col_count
    response = lax.psum(partial_value, ("row", "col"))
    return response * (1.0 / math.sqrt(total_basis * 9 * block_width))


def solution(mesh):
    return jax.shard_map(
        per_device,
        mesh=mesh,
        in_specs=(
            P("row", None, "col", None, None),
            P("row", "col", None),
            P("row", "col", None, None),
            P("row", "col", None, None),
        ),
        out_specs=P(),
        check_vma=False,
    )
```

profile of v0, /device:TPU:0, one launch (start us, length us, event | category | flops | bytes accessed | tf_op | source)
XLA Modules:
  0.0 180.9 jit_solution(1390845295951888833)
XLA Ops:
  0.0 0.0 copy-start
  0.0 1.7 copy.15
  1.7 0.0 copy-start.3
  1.7 1.4 collective-permute-start.1
  3.2 5.6 %collective-permute-start = (bf16[1,1,128,3200]{2,3,1,0:T(8,128)(2,1)S(1)}, bf16[1,1,128,3200]{2,3,1,0:T(8,128)(2,1)S(1)}, u32[]{:S(2)}, u32[]{:S(2)}) collective-permute-start(bf16[1,1,128,3200]{2,3,1,0:T(8,128)(2,1)S(1)} %copy.15), channel_id=1, source_target_pairs={{0,4},{4,8},{8,12},{12,16},{16,20},{20,24},{24,28},{1,5},{5,9},{9,... | collective-permute-start | bytes 2457608 | tf_op jit(solution)/shard_map/ppermute | solution.py:17
  8.7 16.3 %collective-permute-done.1 = bf16[1,1,128,3200]{2,3,1,0:T(8,128)(2,1)S(1)} collective-permute-done((bf16[1,1,128,3200]{2,3,1,0:T(8,128)(2,1)S(1)}, bf16[1,1,128,3200]{2,3,1,0:T(8,128)(2,1)S(1)}, u32[]{:S(2)}, u32[]{:S(2)}) %collective-permute-start.1) | collective-permute-done | bytes 819232 | tf_op jit(solution)/shard_map/ppermute | solution.py:19
  25.0 0.0 copy-start.4
  25.0 17.7 %collective-permute-done = bf16[1,1,128,3200]{2,3,1,0:T(8,128)(2,1)S(1)} collective-permute-done((bf16[1,1,128,3200]{2,3,1,0:T(8,128)(2,1)S(1)}, bf16[1,1,128,3200]{2,3,1,0:T(8,128)(2,1)S(1)}, u32[]{:S(2)}, u32[]{:S(2)}) %collective-permute-start) | collective-permute-done | bytes 819232 | tf_op jit(solution)/shard_map/ppermute | solution.py:17
  42.7 0.0 copy-done.4
  42.7 0.0 copy-start.5
  42.7 1.7 pad_maximum_fusion
  44.4 0.0 copy-done.5
  44.4 1.3 collective-permute-start.3
  45.7 0.0 copy-done.3
  45.7 2.6 %copy.13 = bf16[1,8,1,128,1152]{3,4,2,0,1:T(8,128)(2,1)} copy(bf16[1,8,1,128,1152]{4,3,2,1,0:T(8,128)(2,1)S(1)} %copy-done.3) | data formatting | bytes 4718592 | tf_op args[0]
  48.3 0.0 copy-start.12
  48.3 6.0 %all-to-all-start = ((bf16[1,8,1,128,1152]{3,4,2,0,1:T(8,128)(2,1)}), bf16[1,8,1,128,1152]{3,4,2,0,1:T(8,128)(2,1)S(1)}, u32[]{:S(2)}, u32[]{:S(2)}) async-start(bf16[1,8,1,128,1152]{3,4,2,0,1:T(8,128)(2,1)} %copy.13), calls=%async_computation | async-start | bytes 4718592 | tf_op jit(solution)/shard_map/all_to_all | solution.py:38
  54.3 4.2 %collective-permute-start.2 = (bf16[3,1,128,3200]{2,3,1,0:T(8,128)(2,1)}, bf16[3,1,128,3200]{2,3,1,0:T(8,128)(2,1)}, u32[]{:S(2)}, u32[]{:S(2)}) collective-permute-start(bf16[3,1,128,3200]{2,3,1,0:T(8,128)(2,1)} %pad_maximum_fusion), channel_id=1, source_target_pairs={{0,1},{1,2},{2,3},{4,5},{5,6},{6,7},{8,9},{9,10},{10,11},{12,13},{... | collective-permute-start | bytes 7372808 | tf_op jit(solution)/shard_map/ppermute | solution.py:17
  58.5 0.0 copy-done.12
  58.5 0.1 broadcast_bitcast_fusion
  58.6 1.0 slice.116
  59.6 1.7 slice.100
  61.3 0.0 collective-permute-done.3
  61.3 1.8 fusion.27
  63.1 0.7 slice.119
  63.9 0.7 slice.103
  64.6 0.0 collective-permute-done.2
  64.6 1.8 fusion.26
  66.4 0.7 slice.114
  67.2 0.8 slice.106
  67.9 0.7 slice.98
  68.7 41.0 %all-to-all-done = bf16[1,8,1,128,1152]{3,4,2,0,1:T(8,128)(2,1)S(1)} async-done(((bf16[1,8,1,128,1152]{3,4,2,0,1:T(8,128)(2,1)}), bf16[1,8,1,128,1152]{3,4,2,0,1:T(8,128)(2,1)S(1)}, u32[]{:S(2)}, u32[]{:S(2)}) %all-to-all-start) | async-done | bytes 2359328 | tf_op jit(solution)/shard_map/all_to_all | solution.py:38
  109.7 2.6 %copy.14 = bf16[1,8,1,128,1152]{4,3,1,2,0:T(8,128)(2,1)} copy(bf16[1,8,1,128,1152]{3,4,2,0,1:T(8,128)(2,1)S(1)} %all-to-all-done) | data formatting | bytes 4718592 | tf_op jit(solution)/shard_map/all_to_all | solution.py:38
  112.3 3.3 %bitcast_multiply_fusion = bf16[1024,1152]{1,0:T(8,128)(2,1)} fusion(bf16[1,8,1,128,1152]{4,3,1,2,0:T(8,128)(2,1)} %copy.14, bf16[1152]{0:T(1024)(128)(2,1)S(1)} %broadcast_bitcast_fusion), kind=kLoop, calls=%fused_computation.15 | loop fusion | flops 1179648 | bytes 4720896 | tf_op jit(solution)/shard_map/mul | solution.py:58
  115.6 0.0 copy-done
  115.6 2.2 %fusion.4 = bf16[8,1,1,128,1152]{3,4,0,2,1:T(8,128)(2,1)} fusion(bf16[1,8,1,128,1152]{3,4,2,0,1:T(8,128)(2,1)S(1)} %all-to-all-done, bf16[1152]{0:T(1024)(128)(2,1)S(1)} %broadcast_bitcast_fusion, bf16[1,1,128,128]{3,2,1,0:T(8,128)(2,1)S(1)} %copy-done), kind=kOutput, calls=%fused_computation.12 | convolution fusion | flops 304349184 | bytes 4753664 | tf_op jit(solution)/shard_map/ji,pabiw->pabjw/dot_general | solution.py:39
  117.8 4.3 %copy.19 = bf16[8,1,1,128,1152]{4,3,0,2,1:T(8,128)(2,1)} copy(bf16[8,1,1,128,1152]{3,4,0,2,1:T(8,128)(2,1)} %fusion.4) | data formatting | bytes 4718592 | tf_op jit(solution)/shard_map/mul | solution.py:59
  122.1 0.0 copy-start.2
  122.1 0.0 copy-start.9
  122.1 3.1 %copy.20 = bf16[1,8,128,1152]{3,1,2,0:T(8,128)(2,1)S(1)} copy(bf16[1,8,128,1152]{3,2,1,0:T(8,128)(2,1)} %bitcast.64) | data formatting | bytes 4718592
  125.2 0.0 copy-done.2
  125.2 0.0 copy-done.9
  125.3 0.0 copy-start.6
  125.3 0.8 fusion.6
  126.0 0.2 copy-done.6
  126.2 0.0 copy-start.11
  126.2 0.8 fusion.14
  127.0 0.2 copy-done.11
  127.2 0.8 convolution_add_fusion.6
  128.0 0.2 copy-done.8
  128.1 0.8 convolution_add_fusion.5
  128.9 0.2 copy-done.10
  129.1 0.8 convolution_add_fusion.4
  129.9 0.8 convolution_add_fusion.3
  130.7 0.0 copy-start.7
  130.7 0.8 convolution_add_fusion.2
  131.5 0.2 copy-done.7
  131.7 0.8 convolution_add_fusion.1
  132.5 2.2 %fusion.1 = bf16[1024,1152]{1,0:T(8,128)(2,1)} fusion(f32[1024,1152]{1,0:T(8,128)S(1)} %fusion.6, f32[1024,1152]{1,0:T(8,128)S(1)} %convolution_add_fusion.1, bf16[128,1152]{0,1:T(8,128)(2,1)S(1)} %bitcast.74, bf16[1024,1152]{1,0:T(8,128)(2,1)S(1)} %copy-done.2), kind=kOutput, calls=%fused_computation.8 | convolution fusion | flops 305528832 | bytes 12353536 | tf_op jit(solution)/shard_map/dot_general | solution.py:69
  134.7 4.1 %reshape.69 = bf16[8,147456]{1,0:T(8,128)(2,1)} reshape(bf16[1024,1152]{1,0:T(8,128)(2,1)} %fusion.1) | data formatting | bytes 4718592 | tf_op jit(solution)/shard_map/reshape | solution.py:70
  138.8 3.3 %fusion.28 = f32[8,8]{1,0:T(8,128)S(1)} fusion(bf16[8,147456]{1,0:T(8,128)(2,1)} %reshape.69, bf16[8,147456]{1,0:T(8,128)(2,1)S(1)} %bitcast.63), kind=kOutput, calls=%fused_computation.46 | convolution fusion | flops 18874368 | bytes 4718848 | tf_op jit(solution)/shard_map/dot_general | solution.py:72
  142.1 38.2 %psum.7 = f32[8,8]{1,0:T(8,128)S(1)} all-reduce(f32[8,8]{1,0:T(8,128)S(1)} %fusion.28), channel_id=1, replica_groups=mesh['row'=8,'col'=4] {'row','col'}, use_global_device_ids=true, to_apply=%region_0.1 | all-reduce | flops 64 | bytes 512 | tf_op jit(solution)/shard_map/psum | solution.py:76
  180.3 0.6 broadcast_multiply_fusion
  180.9 0.0 copy-done.1
  (6 shorter events, 0.1 us)
Async XLA Ops:
  0.0 115.6 %copy-start = (bf16[1,1,128,128]{3,2,1,0:T(8,128)(2,1)S(1)}, bf16[1,1,128,128]{3,2,1,0:T(8,128)(2,1)}, u32[]{:S(2)}) copy-start(bf16[1,1,128,128]{3,2,1,0:T(8,128)(2,1)} %param.7) | copy-start | bytes 98308
  1.7 44.0 %copy-start.3 = (bf16[1,8,1,128,1152]{4,3,2,1,0:T(8,128)(2,1)S(1)}, bf16[1,8,1,128,1152]{4,3,2,1,0:T(8,128)(2,1)}, u32[]{:S(2)}) copy-start(bf16[1,8,1,128,1152]{4,3,2,1,0:T(8,128)(2,1)} %param.4) | copy-start | bytes 7077892
  1.7 23.2 %collective-permute-start.1 = (bf16[1,1,128,3200]{2,3,1,0:T(8,128)(2,1)S(1)}, bf16[1,1,128,3200]{2,3,1,0:T(8,128)(2,1)S(1)}, u32[]{:S(2)}, u32[]{:S(2)}) collective-permute-start(bf16[1,1,128,3200]{2,3,1,0:T(8,128)(2,1)S(1)} %copy.15), channel_id=1, source_target_pairs={{4,0},{8,4},{12,8},{16,12},{20,16},{24,20},{28,24},{5,1},{9,5},{13... | collective-permute-start | bytes 2457608 | tf_op jit(solution)/shard_map/ppermute | solution.py:19
  3.2 39.5 %collective-permute-start = (bf16[1,1,128,3200]{2,3,1,0:T(8,128)(2,1)S(1)}, bf16[1,1,128,3200]{2,3,1,0:T(8,128)(2,1)S(1)}, u32[]{:S(2)}, u32[]{:S(2)}) collective-permute-start(bf16[1,1,128,3200]{2,3,1,0:T(8,128)(2,1)S(1)} %copy.15), channel_id=1, source_target_pairs={{0,4},{4,8},{8,12},{12,16},{16,20},{20,24},{24,28},{1,5},{5,9},{9,... | collective-permute-start | bytes 2457608 | tf_op jit(solution)/shard_map/ppermute | solution.py:17
  25.0 17.7 %copy-start.4 = (bf16[1,1,128,3200]{2,3,1,0:T(8,128)(2,1)}, bf16[1,1,128,3200]{2,3,1,0:T(8,128)(2,1)S(1)}, u32[]{:S(2)}) copy-start(bf16[1,1,128,3200]{2,3,1,0:T(8,128)(2,1)S(1)} %collective-permute-done.1) | copy-start | bytes 2457604
  42.7 1.7 copy-start.5
  44.4 16.9 %collective-permute-start.3 = (bf16[3,1,128,3200]{2,3,1,0:T(8,128)(2,1)}, bf16[3,1,128,3200]{2,3,1,0:T(8,128)(2,1)}, u32[]{:S(2)}, u32[]{:S(2)}) collective-permute-start(bf16[3,1,128,3200]{2,3,1,0:T(8,128)(2,1)} %pad_maximum_fusion), channel_id=1, source_target_pairs={{1,0},{2,1},{3,2},{5,4},{6,5},{7,6},{9,8},{10,9},{11,10},{13,12},{... | collective-permute-start | bytes 7372808 | tf_op jit(solution)/shard_map/ppermute | solution.py:19
  48.3 10.2 %copy-start.12 = (s32[1,1,9]{2,1,0:T(1,128)S(1)}, s32[1,1,9]{2,1,0:T(1,128)}, u32[]{:S(2)}) copy-start(s32[1,1,9]{2,1,0:T(1,128)} %param.5) | copy-start | bytes 112
  48.3 61.4 %all-to-all-start = ((bf16[1,8,1,128,1152]{3,4,2,0,1:T(8,128)(2,1)}), bf16[1,8,1,128,1152]{3,4,2,0,1:T(8,128)(2,1)S(1)}, u32[]{:S(2)}, u32[]{:S(2)}) async-start(bf16[1,8,1,128,1152]{3,4,2,0,1:T(8,128)(2,1)} %copy.13), calls=%async_computation | async-start | bytes 4718592 | tf_op jit(solution)/shard_map/all_to_all | solution.py:38
  54.3 10.4 %collective-permute-start.2 = (bf16[3,1,128,3200]{2,3,1,0:T(8,128)(2,1)}, bf16[3,1,128,3200]{2,3,1,0:T(8,128)(2,1)}, u32[]{:S(2)}, u32[]{:S(2)}) collective-permute-start(bf16[3,1,128,3200]{2,3,1,0:T(8,128)(2,1)} %pad_maximum_fusion), channel_id=1, source_target_pairs={{0,1},{1,2},{2,3},{4,5},{5,6},{6,7},{8,9},{9,10},{10,11},{12,13},{... | collective-permute-start | bytes 7372808 | tf_op jit(solution)/shard_map/ppermute | solution.py:17
  122.1 3.1 %copy-start.2 = (bf16[1024,1152]{1,0:T(8,128)(2,1)S(1)}, bf16[1024,1152]{1,0:T(8,128)(2,1)}, u32[]{:S(2)}) copy-start(bf16[1024,1152]{1,0:T(8,128)(2,1)} %bitcast_multiply_fusion) | copy-start | bytes 7077892
  122.1 3.1 %copy-start.9 = (bf16[128,3,3,128]{0,3,2,1:T(8,128)(2,1)S(1)}, bf16[128,3,3,128]{0,3,2,1:T(8,128)(2,1)}, u32[]{:S(2)}) copy-start(bf16[128,3,3,128]{0,3,2,1:T(8,128)(2,1)} %slice.119) | copy-start | bytes 884740
  125.3 1.0 copy-start.6
  126.2 1.0 copy-start.11
  127.2 1.0 copy-start.8
  128.1 1.0 copy-start.10
  130.7 1.0 copy-start.7
  134.7 46.2 %copy-start.1 = (bf16[1,1,128,128]{3,2,1,0:T(8,128)(2,1)S(1)}, bf16[1,1,128,128]{3,2,1,0:T(8,128)(2,1)}, u32[]{:S(2)}) copy-start(bf16[1,1,128,128]{3,2,1,0:T(8,128)(2,1)} %param.7) | copy-start | bytes 98308
where the time goes:
time: 182 us; the launch traced here: 181 us
  waiting for transfers between devices  75 us (41%)
  blocking collectives  38.2 us (21%)
  local copies, waits for them, and re-layouts  29.5 us (16%)
  starting transfers between devices  18.5 us (10%)
  matrix products  13.9 us (8%)
  other arithmetic  5.66 us (3%)
    all_to_all x1, waiting for transfers between devices, per_device(): lax.all_to_all(tensor_ri, 'row', split_axis=1, concat_axis=0, tiled=True)  41 us
    psum x1, blocking collectives, per_device(): response = lax.psum(partial_value, ('row', 'col'))  38.2 us
    ppermute x2, waiting for transfers between devices, extended(): lax.ppermute(tail, axis, [(i, (i + 1) % count) for i in range(ends)])  17.7 us
    ppermute x2, waiting for transfers between devices, extended(): lax.ppermute(head, axis, [((i + 1) % count, i) for i in range(ends)])  16.3 us
    ppermute x2, starting transfers between devices, extended(): lax.ppermute(tail, axis, [(i, (i + 1) % count) for i in range(ends)])  9.79 us
    dot_general x9, matrix products, per_device(): jnp.dot(tile, windows[source], preferred_element_type=jnp.float32)  8.48 us
    unnamed x29, local copies, waits for them, and re-layouts  8.29 us
    slice x9, local copies, waits for them, and re-layouts, window_of(): picked = grid_band[:, 2 - src_row:5 - src_row, 2 - src_col:5 - src_col, :]  6.45 us
  transfers between devices with their start and end apart: 5, of which 3 were waited for; matrix products, arithmetic and copies ran while one was open for 7% of the time, Pallas kernels for 0%

commit v1 on v0

v1 whole, which is shorter than its diff:
```python
import functools
import math

import jax
import jax.numpy as jnp
from jax import lax
from jax.experimental import pallas as pl
from jax.experimental.pallas import tpu as pltpu
from jax.sharding import PartitionSpec as P

MESH = pl.DeviceIdType.MESH
NT = (((1,), (1,)), ((), ()))


def kernel(rows, cols, width, scale, mask_ref, occ_ref, tensor_ref, green_ref, out_ref,
           held, half, pairs, part, row_sums, col_sums,
           own_sem, own_green_sem, send_sem, recv_sem, green_send, green_recv,
           row_send, row_recv, col_send, col_recv):
    r = lax.axis_index("row")
    c = lax.axis_index("col")
    bits = (rows - 1).bit_length()

    def partner(step):
        other = 0
        for bit in range(bits):
            other = other + (1 << bit) * ((r // (1 << bit) + step // (1 << bit)) % 2)
        return other

    def at_lane(block):
        return pl.multiple_of(block * width, width)

    def spans(col, fn):
        inner = (col > 0) & (col < cols - 1)

        @pl.when(inner)
        def _():
            fn(0, 3)

        @pl.when(col == 0)
        def _():
            fn(1, 2)

        @pl.when(col == cols - 1)
        def _():
            fn(0, 2)

    def tensor_copy(src_row, dst_row, step, a, first, count):
        lanes = pl.ds((3 * a + first) * width, count * width)
        return pltpu.make_async_remote_copy(
            src_ref=tensor_ref.at[0, dst_row, 0, :, lanes],
            dst_ref=held.at[src_row, :, lanes],
            send_sem=send_sem.at[step, a],
            recv_sem=recv_sem.at[step, a],
            device_id=(dst_row, c),
            device_id_type=MESH,
        )

    def green_copy(ap, bp, a, first, count, target):
        slot = 3 * ap + bp
        band = 5 * (a - ap + 2) + (first - bp + 2)
        return pltpu.make_async_remote_copy(
            src_ref=green_ref.at[0, 0, :, pl.ds(band * width, count * width)],
            dst_ref=pairs.at[pl.ds(slot * width, width), pl.ds((3 * a + first) * width, count * width)],
            send_sem=green_send.at[slot, a],
            recv_sem=green_recv.at[slot, a],
            device_id=target,
            device_id_type=MESH,
        )

    def row_ok(row):
        return (row >= 0) & (row < rows)

    def col_ok(col):
        return (col >= 0) & (col < cols)

    def each_green_sent(fn):
        for ap in range(3):
            for bp in range(3):
                if ap == 1 and bp == 1:
                    continue
                to_row, to_col = r + 1 - ap, c + 1 - bp

                @pl.when(row_ok(to_row) & col_ok(to_col))
                def _():
                    for a in range(3):
                        @pl.when(row_ok(to_row + a - 1))
                        def _():
                            spans(to_col, lambda first, count: fn(
                                green_copy(ap, bp, a, first, count, (to_row, to_col))))

    def each_green_received(fn):
        for ap in range(3):
            for bp in range(3):
                if ap == 1 and bp == 1:
                    continue

                @pl.when(row_ok(r + ap - 1) & col_ok(c + bp - 1))
                def _():
                    for a in range(3):
                        @pl.when(row_ok(r + a - 1))
                        def _():
                            spans(c, lambda first, count: fn(
                                green_copy(ap, bp, a, first, count, (r, c))))

    def each_tensor_sent(step, fn):
        other = partner(step)
        for a in range(3):
            @pl.when(row_ok(other + a - 1))
            def _():
                spans(c, lambda first, count: fn(tensor_copy(r, other, step, a, first, count)))

    def each_tensor_received(step, fn):
        other = partner(step)
        for a in range(3):
            @pl.when(row_ok(r + a - 1))
            def _():
                spans(c, lambda first, count: fn(tensor_copy(other, r, step, a, first, count)))

    own = pltpu.make_async_copy(tensor_ref.at[0, r, 0], held.at[r], own_sem)
    own.start()
    own_green = []
    for a in range(3):
        band = 5 * (a + 1) + 1
        own_green.append(pltpu.make_async_copy(
            green_ref.at[0, 0, :, pl.ds(band * width, 3 * width)],
            pairs.at[pl.ds(4 * width, width), pl.ds(3 * a * width, 3 * width)],
            own_green_sem.at[a]))
        own_green[a].start()

    barrier = pltpu.get_barrier_semaphore()

    def greet(row, col):
        pl.semaphore_signal(barrier, inc=1, device_id=(row, col), device_id_type=MESH)

    @pl.loop(1, rows)
    def _(step):
        greet(partner(step), c)

    @pl.loop(1, cols)
    def _(step):
        greet(r, (c + step) % cols)

    corners = 0
    for dr in (-1, 1):
        for dc in (-1, 1):
            there = row_ok(r + dr) & col_ok(c + dc)
            corners = corners + there.astype(jnp.int32)

            @pl.when(there)
            def _():
                greet(r + dr, c + dc)

    pl.semaphore_wait(barrier, rows - 1 + cols - 1 + corners)

    each_green_sent(lambda copy: copy.start())

    @pl.loop(1, rows)
    def _(step):
        each_tensor_sent(rows - step, lambda copy: copy.start())

    @pl.loop(1, rows)
    def _(step):
        other = partner(step)
        for a in range(3):
            for b in range(3):
                @pl.when(jnp.logical_not(row_ok(r + a - 1) & col_ok(c + b - 1)))
                def _():
                    held[other, :, pl.ds((3 * a + b) * width, width)] = jnp.zeros((width, width), held.dtype)

    for copy in own_green:
        copy.wait()
    each_green_received(lambda copy: copy.wait_recv())

    keep = []
    for k in range(9):
        a, b = k // 3, k % 3
        inside = (row_ok(r + a - 1) & col_ok(c + b - 1)).astype(jnp.int32)
        keep.append((mask_ref[0, 0, k] == 1).astype(jnp.int32) * inside)
    for kp in range(9):
        for k in range(9):
            both = jnp.full((width, width), keep[kp] * keep[k], jnp.int32)
            tile = pairs[kp * width:(kp + 1) * width, k * width:(k + 1) * width].astype(jnp.float32)
            pairs[kp * width:(kp + 1) * width, k * width:(k + 1) * width] = jnp.where(
                both == 1, tile, 0.0).astype(pairs.dtype)

    own.wait()
    occ = occ_ref[0, 0].astype(jnp.float32)

    def pair_row(left, right):
        gram = lax.dot_general(half[left], held[right], NT, preferred_element_type=jnp.float32)
        return jnp.sum(gram * occ, axis=0, keepdims=True)

    @pl.loop(0, rows)
    def _(step):
        p = partner(step)

        @pl.when(step > 0)
        def _():
            each_tensor_received(step, lambda copy: copy.wait_recv())

        for a in range(3):
            lanes = slice(3 * a * width, 3 * (a + 1) * width)
            half[p, :, lanes] = jnp.dot(
                held[p], pairs[:, lanes], preferred_element_type=jnp.float32).astype(half.dtype)

        @pl.loop(0, step + 1)
        def _(earlier):
            q = partner(earlier)
            part[p, pl.ds(q, 1), :] = pair_row(p, q)
            part[q, pl.ds(p, 1), :] = pair_row(q, p)

    lanes_total = row_sums.shape[-1]
    row_sums[r] = jnp.zeros(row_sums.shape[1:], jnp.float32)
    row_sums[r, :, 0:rows] = jnp.sum(part[...], axis=2)

    def row_copy(step, src, dst):
        return pltpu.make_async_remote_copy(
            src_ref=row_sums.at[src], dst_ref=row_sums.at[src],
            send_sem=row_send.at[step], recv_sem=row_recv.at[step],
            device_id=(dst, c), device_id_type=MESH)

    def col_copy(step, src, dst):
        return pltpu.make_async_remote_copy(
            src_ref=col_sums.at[src], dst_ref=col_sums.at[src],
            send_sem=col_send.at[step], recv_sem=col_recv.at[step],
            device_id=(r, dst), device_id_type=MESH)

    @pl.loop(1, rows)
    def _(step):
        row_copy(step, r, partner(step)).start()

    @pl.loop(1, rows)
    def _(step):
        row_copy(step, partner(step), r).wait_recv()

    col_sums[c] = jnp.sum(row_sums[...], axis=0)

    @pl.loop(1, cols)
    def _(step):
        col_copy(step, c, (c + step) % cols).start()

    @pl.loop(1, cols)
    def _(step):
        col_copy(step, (c + cols - step) % cols, c).wait_recv()

    out_ref[...] = (jnp.sum(col_sums[...], axis=0) * scale)[:, 0:rows]

    each_green_sent(lambda copy: copy.wait_send())

    @pl.loop(1, rows)
    def _(step):
        each_tensor_sent(step, lambda copy: copy.wait_send())
        row_copy(step, r, partner(step)).wait_send()

    @pl.loop(1, cols)
    def _(step):
        col_copy(step, c, (c + step) % cols).wait_send()


def per_device(tensor_ri, block_mask, green_virt, green_occ):
    rows = lax.axis_size("row")
    cols = lax.axis_size("col")
    width = green_occ.shape[-1]
    wide = tensor_ri.shape[-1]
    scale = 1.0 / math.sqrt(width * rows * cols * wide)
    lanes = 128
    hbm = pl.BlockSpec(memory_space=pltpu.MemorySpace.HBM)
    dma = pltpu.SemaphoreType.DMA
    return pl.pallas_call(
        functools.partial(kernel, rows, cols, width, scale),
        out_shape=jax.ShapeDtypeStruct((rows, rows), jnp.float32),
        in_specs=[
            pl.BlockSpec(memory_space=pltpu.MemorySpace.SMEM),
            pl.BlockSpec(memory_space=pltpu.MemorySpace.VMEM),
            hbm,
            hbm,
        ],
        out_specs=pl.BlockSpec(memory_space=pltpu.MemorySpace.VMEM),
        scratch_shapes=[
            pltpu.VMEM((rows, width, wide), jnp.bfloat16),
            pltpu.VMEM((rows, width, wide), jnp.bfloat16),
            pltpu.VMEM((wide, wide), jnp.bfloat16),
            pltpu.VMEM((rows, rows, width), jnp.float32),
            pltpu.VMEM((rows, rows, lanes), jnp.float32),
            pltpu.VMEM((cols, rows, lanes), jnp.float32),
            dma,
            dma((3,)),
            dma((rows, 3)),
            dma((rows, 3)),
            dma((9, 3)),
            dma((9, 3)),
            dma((rows,)),
            dma((rows,)),
            dma((cols,)),
            dma((cols,)),
        ],
        compiler_params=pltpu.CompilerParams(
            collective_id=0, has_side_effects=True, vmem_limit_bytes=63 * 1024 * 1024),
    )(block_mask, green_occ, tensor_ri, green_virt)


def solution(mesh):
    return jax.shard_map(
        per_device,
        mesh=mesh,
        in_specs=(
            P("row", None, "col", None, None),
            P("row", "col", None),
            P("row", "col", None, None),
            P("row", "col", None, None),
        ),
        out_specs=P(),
        check_vma=False,
    )
```

time: 182 us -> 91.1 us (0.50)
  Pallas kernels: 0 us -> 89.6 us
  waiting for transfers between devices: 75 us -> 0 us
  blocking collectives: 38.2 us -> 0 us
  local copies, waits for them, and re-layouts: 29.5 us -> 1.28 us
  starting transfers between devices: 18.5 us -> 0 us
  matrix products: 13.9 us -> 0 us
  other arithmetic: 5.66 us -> 0 us
    pallas_call x0 -> x1, Pallas kernels: none -> 89.6 us  [per_device(): pl.pallas_call(functools.partial(kernel, rows, cols, width, scale), out_s...]
    all_to_all x1 -> x0, waiting for transfers between devices: 41 us -> none  [per_device(): lax.all_to_all(tensor_ri, 'row', split_axis=1, concat_axis=0, tiled=True)]
    psum x1 -> x0, blocking collectives: 38.2 us -> none  [per_device(): response = lax.psum(partial_value, ('row', 'col'))]
    ppermute x4 -> x0, waiting for transfers between devices: 34 us -> none  [the longest x2 17.7 us: extended(): lax.ppermute(tail, axis, [(i, (i + 1) % count) for i in range(ends)])]
    dot_general x11 -> x0, matrix products: 13.9 us -> none  [the longest x9 8.48 us: per_device(): jnp.dot(tile, windows[source], preferred_element_type=jnp.float32)]
    ppermute x4 -> x0, starting transfers between devices: 12.5 us -> none  [the longest x2 9.79 us: extended(): lax.ppermute(tail, axis, [(i, (i + 1) % count) for i in range(ends)])]
    slice x11 -> x0, local copies, waits for them, and re-layouts: 10 us -> none  [the longest x9 6.45 us: window_of(): picked = grid_band[:, 2 - src_row:5 - src_row, 2 - src_col:5 - src_col, :]]
    unnamed x29 -> x1, local copies, waits for them, and re-layouts: 8.29 us -> 1.28 us
  transfers between devices with their start and end apart: 5 -> 0, of which waited for: 3 -> 0; matrix products, arithmetic and copies ran while one was open for 7% -> 0% of each run, Pallas kernels for 0% -> 0%
where the time goes in v1:
time: 91.1 us; the launch traced here: 90.9 us
  Pallas kernels  89.6 us (98%)
  local copies, waits for them, and re-layouts  1.28 us (1%)
    pallas_call x1, Pallas kernels, per_device(): pl.pallas_call(functools.partial(kernel, rows, cols, width, scale), out_s...  89.6 us

profile of v1, /device:TPU:0, one launch (start us, length us, event | category | flops | bytes accessed | tf_op | source)
XLA Modules:
  0.0 90.9 jit_solution(1268844064505376304)
XLA Ops:
  0.0 89.6 %shard_map.46 = f32[8,8]{1,0:T(8,128)} custom-call(s32[1,1,9]{2,1,0:T(1,128)} %mask_ref.1, bf16[1,1,128,128]{3,2,1,0:T(8,128)(2,1)} %occ_ref.1, bf16[1,8,1,128,1152]{4,3,2,1,0:T(8,128)(2,1)} %tensor_ref.1, bf16[1,1,128,3200]{3,2,1,0:T(8,128)(2,1)} %green_ref.1), custom_call_target="tpu_custom_call" | custom-call | tf_op jit(solution)/shard_map/pallas_call | solution.py:269
  89.7 1.3 %copy.6 = f32[8,8]{1,0:T(8,128)} copy(f32[8,8]{1,0:T(8,128)} %shard_map.46) | data formatting | bytes 512

commit v2 on v1

--- a/solution.py
+++ b/solution.py
@@ -13,12 +13,14 @@
 
 
 def kernel(rows, cols, width, scale, mask_ref, occ_ref, tensor_ref, green_ref, out_ref,
-           held, half, pairs, part, row_sums, col_sums,
+           held, half, pairs, stage, part, row_sums, col_sums,
            own_sem, own_green_sem, send_sem, recv_sem, green_send, green_recv,
+           stage_send, stage_recv, forward_send,
            row_send, row_recv, col_send, col_recv):
     r = lax.axis_index("row")
     c = lax.axis_index("col")
     bits = (rows - 1).bit_length()
+    wide = 9 * width
 
     def partner(step):
         other = 0
@@ -48,7 +50,7 @@
         lanes = pl.ds((3 * a + first) * width, count * width)
         return pltpu.make_async_remote_copy(
             src_ref=tensor_ref.at[0, dst_row, 0, :, lanes],
-            dst_ref=held.at[src_row, :, lanes],
+            dst_ref=held.at[step, :, lanes],
             send_sem=send_sem.at[step, a],
             recv_sem=recv_sem.at[step, a],
             device_id=(dst_row, c),
@@ -79,8 +81,13 @@
                 if ap == 1 and bp == 1:
                     continue
                 to_row, to_col = r + 1 - ap, c + 1 - bp
-
-                @pl.when(row_ok(to_row) & col_ok(to_col))
+                direct = row_ok(to_row) & col_ok(to_col)
+                if ap != 1:
+                    if bp == 1:
+                        continue
+                    direct = direct & (c % 2 == 1 - bp // 2)
+
+                @pl.when(direct)
                 def _():
                     for a in range(3):
                         @pl.when(row_ok(to_row + a - 1))
@@ -91,7 +98,7 @@
     def each_green_received(fn):
         for ap in range(3):
             for bp in range(3):
-                if ap == 1 and bp == 1:
+                if bp == 1:
                     continue
 
                 @pl.when(row_ok(r + ap - 1) & col_ok(c + bp - 1))
@@ -102,6 +109,60 @@
                             spans(c, lambda first, count: fn(
                                 green_copy(ap, bp, a, first, count, (r, c))))
 
+    low = 1 - c % 2 + (c < 2).astype(jnp.int32)
+    rim_chip = (c < 2) | (c >= cols - 2)
+
+    def each_staged(fn, to):
+        for side in range(2):
+            ap = 2 * side
+            target = r + 1 - ap if to else r
+            source = target + ap - 1
+
+            @pl.when(row_ok(target) & row_ok(source))
+            def _():
+                for a in range(3):
+                    @pl.when(row_ok(target + a - 1))
+                    def _():
+                        def piece(count):
+                            fn(pltpu.make_async_remote_copy(
+                                src_ref=green_ref.at[0, 0, :, pl.ds(
+                                    at_lane(5 * (a - ap + 2) + low), count * width)],
+                                dst_ref=stage.at[side, a, :, pl.ds(0, count * width)],
+                                send_sem=stage_send.at[side, a],
+                                recv_sem=stage_recv.at[side, a],
+                                device_id=(target, c),
+                                device_id_type=MESH))
+
+                        @pl.when(rim_chip)
+                        def _():
+                            piece(3)
+
+                        @pl.when(jnp.logical_not(rim_chip))
+                        def _():
+                            piece(4)
+
+    def each_forwarded(fn):
+        for side in range(2):
+            ap = 2 * side
+            for bp in (0, 2):
+                sibling = c + 1 - bp
+
+                @pl.when(row_ok(r + ap - 1) & (c % 2 == bp // 2))
+                def _():
+                    for a in range(3):
+                        @pl.when(row_ok(r + a - 1))
+                        def _():
+                            spans(sibling, lambda first, count: fn(pltpu.make_async_remote_copy(
+                                src_ref=stage.at[side, a, :, pl.ds(
+                                    at_lane(first - bp + 2 - low), count * width)],
+                                dst_ref=pairs.at[
+                                    pl.ds((3 * ap + bp) * width, width),
+                                    pl.ds((3 * a + first) * width, count * width)],
+                                send_sem=forward_send.at[side, a],
+                                recv_sem=green_recv.at[3 * ap + bp, a],
+                                device_id=(r, sibling),
+                                device_id_type=MESH)))
+
     def each_tensor_sent(step, fn):
         other = partner(step)
         for a in range(3):
@@ -116,7 +177,7 @@
             def _():
                 spans(c, lambda first, count: fn(tensor_copy(other, r, step, a, first, count)))
 
-    own = pltpu.make_async_copy(tensor_ref.at[0, r, 0], held.at[r], own_sem)
+    own = pltpu.make_async_copy(tensor_ref.at[0, r, 0], held.at[0], own_sem)
     own.start()
     own_green = []
     for a in range(3):
@@ -152,23 +213,38 @@
 
     pl.semaphore_wait(barrier, rows - 1 + cols - 1 + corners)
 
+    @pl.loop(rows // 2, rows // 2 + 1)
+    def _(step):
+        each_tensor_sent(step, lambda copy: copy.start())
+
+    each_staged(lambda copy: copy.start(), True)
+
+    @pl.loop(rows // 2 + 1, rows // 2 + 2)
+    def _(step):
+        each_tensor_sent(step, lambda copy: copy.start())
+
     each_green_sent(lambda copy: copy.start())
 
+    @pl.loop(rows // 2 + 2, rows)
+    def _(step):
+        each_tensor_sent(step, lambda copy: copy.start())
+
+    @pl.loop(1, rows // 2)
+    def _(step):
+        each_tensor_sent(step, lambda copy: copy.start())
+
     @pl.loop(1, rows)
     def _(step):
-        each_tensor_sent(rows - step, lambda copy: copy.start())
-
-    @pl.loop(1, rows)
-    def _(step):
-        other = partner(step)
         for a in range(3):
             for b in range(3):
                 @pl.when(jnp.logical_not(row_ok(r + a - 1) & col_ok(c + b - 1)))
                 def _():
-                    held[other, :, pl.ds((3 * a + b) * width, width)] = jnp.zeros((width, width), held.dtype)
+                    held[step, :, pl.ds((3 * a + b) * width, width)] = jnp.zeros((width, width), held.dtype)
 
     for copy in own_green:
         copy.wait()
+    each_staged(lambda copy: copy.wait_recv(), False)
+    each_forwarded(lambda copy: copy.start())
     each_green_received(lambda copy: copy.wait_recv())
 
     keep = []
@@ -179,37 +255,65 @@
     for kp in range(9):
         for k in range(9):
             both = jnp.full((width, width), keep[kp] * keep[k], jnp.int32)
-            tile = pairs[kp * width:(kp + 1) * width, k * width:(k + 1) * width].astype(jnp.float32)
+            if kp in (1, 7):
+                block = jnp.minimum(jnp.maximum(k % 3 + 1 - low, 0), 3)
+                tile = stage[kp // 6, k // 3, :, pl.ds(at_lane(block), width)]
+            else:
+                tile = pairs[kp * width:(kp + 1) * width, k * width:(k + 1) * width]
+            tile = tile.astype(jnp.float32)
             pairs[kp * width:(kp + 1) * width, k * width:(k + 1) * width] = jnp.where(
                 both == 1, tile, 0.0).astype(pairs.dtype)
 
     own.wait()
     occ = occ_ref[0, 0].astype(jnp.float32)
 
-    def pair_row(left, right):
-        gram = lax.dot_general(half[left], held[right], NT, preferred_element_type=jnp.float32)
-        return jnp.sum(gram * occ, axis=0, keepdims=True)
-
-    @pl.loop(0, rows)
-    def _(step):
-        p = partner(step)
-
-        @pl.when(step > 0)
-        def _():
-            each_tensor_received(step, lambda copy: copy.wait_recv())
-
+    def apply_green(start, count):
+        stacked = held[pl.ds(start, count)].reshape(count * width, wide)
         for a in range(3):
             lanes = slice(3 * a * width, 3 * (a + 1) * width)
-            half[p, :, lanes] = jnp.dot(
-                held[p], pairs[:, lanes], preferred_element_type=jnp.float32).astype(half.dtype)
-
-        @pl.loop(0, step + 1)
-        def _(earlier):
-            q = partner(earlier)
-            part[p, pl.ds(q, 1), :] = pair_row(p, q)
-            part[q, pl.ds(p, 1), :] = pair_row(q, p)
-
-    lanes_total = row_sums.shape[-1]
+            half[pl.ds(start, count), :, lanes] = jnp.dot(
+                stacked, pairs[:, lanes], preferred_element_type=jnp.float32
+            ).astype(half.dtype).reshape(count, width, 3 * width)
+
+    def pair_rows(left, left_count, right, right_count):
+        gram = lax.dot_general(
+            half[pl.ds(left, left_count)].reshape(left_count * width, wide),
+            held[pl.ds(right, right_count)].reshape(right_count * width, wide),
+            NT, preferred_element_type=jnp.float32)
+        for i in range(left_count):
+            for j in range(right_count):
+                tile = gram[i * width:(i + 1) * width, j * width:(j + 1) * width]
+                part[partner(left + i), pl.ds(partner(right + j), 1), :] = jnp.sum(
+                    tile * occ, axis=0, keepdims=True)
+
+    def arrive(step):
+        each_tensor_received(step, lambda copy: copy.wait_recv())
+
+    if rows <= 8:
+        for start in range(0, rows, 2):
+            for step in range(max(start, 1), start + 2):
+                arrive(step)
+            apply_green(start, 2)
+            pair_rows(start, 2, 0, start + 2)
+            if start:
+                pair_rows(0, start, start, 2)
+    else:
+        @pl.loop(0, rows // 2)
+        def _(group):
+            start = 2 * group
+
+            @pl.when(group > 0)
+            def _():
+                arrive(start)
+
+            arrive(start + 1)
+            apply_green(start, 2)
+
+            @pl.loop(0, group + 1)
+            def _(earlier):
+                pair_rows(start, 2, 2 * earlier, 2)
+                pair_rows(2 * earlier, 2, start, 2)
+
     row_sums[r] = jnp.zeros(row_sums.shape[1:], jnp.float32)
     row_sums[r, :, 0:rows] = jnp.sum(part[...], axis=2)
 
@@ -246,6 +350,8 @@
     out_ref[...] = (jnp.sum(col_sums[...], axis=0) * scale)[:, 0:rows]
 
     each_green_sent(lambda copy: copy.wait_send())
+    each_staged(lambda copy: copy.wait_send(), True)
+    each_forwarded(lambda copy: copy.wait_send())
 
     @pl.loop(1, rows)
     def _(step):
@@ -280,6 +386,7 @@
             pltpu.VMEM((rows, width, wide), jnp.bfloat16),
             pltpu.VMEM((rows, width, wide), jnp.bfloat16),
             pltpu.VMEM((wide, wide), jnp.bfloat16),
+            pltpu.VMEM((2, 3, width, 4 * width), jnp.bfloat16),
             pltpu.VMEM((rows, rows, width), jnp.float32),
             pltpu.VMEM((rows, rows, lanes), jnp.float32),
             pltpu.VMEM((cols, rows, lanes), jnp.float32),
@@ -289,6 +396,9 @@
             dma((rows, 3)),
             dma((9, 3)),
             dma((9, 3)),
+            dma((2, 3)),
+            dma((2, 3)),
+            dma((2, 3)),
             dma((rows,)),
             dma((rows,)),
             dma((cols,)),

time: 91.1 us -> 70.3 us (0.77)
  Pallas kernels: 89.6 us -> 68.8 us
    pallas_call x1, Pallas kernels: 89.6 us -> 68.8 us  [per_device(): pl.pallas_call(functools.partial(kernel, rows, cols, width, scale), out_s...]
where the time goes in v2:
time: 70.3 us; the launch traced here: 70.1 us
  Pallas kernels  68.8 us (98%)
  local copies, waits for them, and re-layouts  1.28 us (2%)
    pallas_call x1, Pallas kernels, per_device(): pl.pallas_call(functools.partial(kernel, rows, cols, width, scale), out_s...  68.8 us

profile of v2, /device:TPU:0, one launch (start us, length us, event | category | flops | bytes accessed | tf_op | source)
XLA Modules:
  0.0 70.1 jit_solution(2124896250500849546)
XLA Ops:
  0.0 68.8 %shard_map.46 = f32[8,8]{1,0:T(8,128)} custom-call(s32[1,1,9]{2,1,0:T(1,128)} %mask_ref.1, bf16[1,1,128,128]{3,2,1,0:T(8,128)(2,1)} %occ_ref.1, bf16[1,8,1,128,1152]{4,3,2,1,0:T(8,128)(2,1)} %tensor_ref.1, bf16[1,1,128,3200]{3,2,1,0:T(8,128)(2,1)} %green_ref.1), custom_call_target="tpu_custom_call" | custom-call | tf_op jit(solution)/shard_map/pallas_call | solution.py:375
  68.8 1.3 %copy.6 = f32[8,8]{1,0:T(8,128)} copy(f32[8,8]{1,0:T(8,128)} %shard_map.46) | data formatting | bytes 512

commit v3 on v2

--- a/solution.py
+++ b/solution.py
@@ -219,18 +219,19 @@
 
     each_staged(lambda copy: copy.start(), True)
 
+    @pl.loop(1, 2)
+    def _(step):
+        each_tensor_sent(step, lambda copy: copy.start())
+
     @pl.loop(rows // 2 + 1, rows // 2 + 2)
     def _(step):
         each_tensor_sent(step, lambda copy: copy.start())
 
     each_green_sent(lambda copy: copy.start())
 
-    @pl.loop(rows // 2 + 2, rows)
-    def _(step):
-        each_tensor_sent(step, lambda copy: copy.start())
-
-    @pl.loop(1, rows // 2)
-    def _(step):
+    @pl.loop(2, rows // 2)
+    def _(step):
+        each_tensor_sent(rows // 2 + step, lambda copy: copy.start())
         each_tensor_sent(step, lambda copy: copy.start())
 
     @pl.loop(1, rows)

time: 70.3 us -> 69.7 us (level)
  no operation moved by 1% of the time
where the time goes in v3:
time: 69.7 us; the launch traced here: 69.5 us
  Pallas kernels  68.2 us (98%)
  local copies, waits for them, and re-layouts  1.28 us (2%)
    pallas_call x1, Pallas kernels, per_device(): pl.pallas_call(functools.partial(kernel, rows, cols, width, scale), out_s...  68.2 us

profile of v3, /device:TPU:0, one launch (start us, length us, event | category | flops | bytes accessed | tf_op | source)
XLA Modules:
  0.0 69.5 jit_solution(5508246419863805911)
XLA Ops:
  0.0 68.2 %shard_map.46 = f32[8,8]{1,0:T(8,128)} custom-call(s32[1,1,9]{2,1,0:T(1,128)} %mask_ref.1, bf16[1,1,128,128]{3,2,1,0:T(8,128)(2,1)} %occ_ref.1, bf16[1,8,1,128,1152]{4,3,2,1,0:T(8,128)(2,1)} %tensor_ref.1, bf16[1,1,128,3200]{3,2,1,0:T(8,128)(2,1)} %green_ref.1), custom_call_target="tpu_custom_call" | custom-call | tf_op jit(solution)/shard_map/pallas_call | solution.py:376
  68.2 1.3 %copy.6 = f32[8,8]{1,0:T(8,128)} copy(f32[8,8]{1,0:T(8,128)} %shard_map.46) | data formatting | bytes 512
